TPU v7x, 128 devices: a whole 4x4x4 slice. The times are simulated.
128 devices in a mesh: row: 16 (over y, x), col: 8 (over z, core).
Axes of the slice: x: 4, y: 4, z: 4, core: 2. Of those that a mesh axis runs over, the one named last changes fastest.
Arguments:
- x_blocks: bfloat16 [128, 16, 256, 256], P('row', 'col'), may hold values from -0.75 to 0.75, as said below
- x_cols: int32 [128, 16], P('row', 'col'), may hold values from -1 to 127, as said below
- out_cols: int32 [128, 32], P('row', 'col'), may hold values from 0 to 127, as said below
- branch_flag: int32 [128], P('row'), may hold values from 0 to 1
Outputs:
- purified: bfloat16 [128, 32, 256, 256], P('row', 'col')
- trace: float32 [1], replicated
Inputs may be any that keep to these rules, and one draw needn't show every extreme that they name: `x_cols`: slot c * 2 + s of block row i holds -1 or a block column in c * 16 to (c + 1) * 16 - 1; the filled columns of one block row are distinct. The pattern is symmetric: block row i names column j exactly when block row j names column i. The rows of one device hold at most 13 filled slots together, and the rows of some device hold exactly 13. `x_blocks`: the stored block of position (j, i) is the transpose of the stored block of position (i, j); stored diagonal blocks are symmetric. `out_cols`: slot c * 4 + o of block row i holds a block column in c * 16 to (c + 1) * 16 - 1, distinct within one block row; column i is always among the slots of block row i. `branch_flag`: entry i is 0 where block row i takes X times X, 1 where it takes 2 X minus X times X.
All inputs are finite; a program needn't handle non-finite values.
Results may differ from a plain program's by a relative error of at most 0.001.
Values may be sent and summed in bfloat16 or wider, within the bound.
A program may use at most 192 MiB of HBM per device.

v0:
```python
import jax
import jax.numpy as jnp
from jax import lax
from jax.sharding import PartitionSpec as P


def per_device(x_blocks, x_cols, out_cols, branch_flag):
    rows = x_cols.shape[0]
    slots = x_cols.shape[1]
    block = x_blocks.shape[-1]
    kept = out_cols.shape[1]
    filled = x_cols >= 0
    cleared = jnp.where(filled[:, :, None, None], x_blocks, jnp.zeros_like(x_blocks))
    flag_rows = branch_flag == 1
    base_row = lax.axis_index("row") * rows
    left_blocks, left_cols = (
        lax.all_gather(cleared, "col", axis=1, tiled=True),
        lax.all_gather(x_cols, "col", axis=1, tiled=True),
    )
    right_blocks, right_cols = (
        lax.all_gather(cleared, "row", axis=0, tiled=True),
        lax.all_gather(x_cols, "row", axis=0, tiled=True),
    )

    def fetch(local):
        entries = left_cols[local]
        live = entries >= 0
        source_rows = jnp.where(live, entries, 0)
        fetched = right_blocks[source_rows]
        fetched_cols = jnp.where(live[:, None], right_cols[source_rows], -1)
        return (left_blocks[local], fetched, fetched_cols)

    def one_row(local):
        lhs, fetched, fetched_cols = fetch(local)
        width = fetched_cols.shape[0] * fetched_cols.shape[1]
        products = jnp.einsum("exy,esyz->esxz", lhs, fetched, preferred_element_type=jnp.float32)
        targets = out_cols[local]
        match = (
            (fetched_cols[None, :, :] == targets[:, None, None])
            .astype(jnp.float32)
            .reshape(kept, width)
        )
        square = jnp.dot(
            match, products.reshape(width, block * block), precision=lax.Precision.HIGHEST
        ).reshape(kept, block, block)
        own_match = (x_cols[local][None, :] == targets[:, None]).astype(jnp.float32)
        own_blocks = cleared[local].astype(jnp.float32).reshape(slots, block * block)
        own = jnp.dot(own_match, own_blocks, precision=lax.Precision.HIGHEST).reshape(
            kept, block, block
        )
        result = jnp.where(flag_rows[local], 2.0 * own - square, square)
        diag_here = (targets == base_row + local).astype(jnp.float32)
        part = jnp.sum(diag_here * jnp.trace(result, axis1=1, axis2=2))
        return (result.astype(jnp.bfloat16), part)

    purified, parts = lax.map(one_row, jnp.arange(rows, dtype=jnp.int32))
    trace_total = lax.psum(jnp.sum(parts), ("row", "col"))
    return (purified, trace_total.reshape(1))


def solution(mesh):
    in_specs = (P("row", "col", None, None), P("row", "col"), P("row", "col"), P("row"))
    out_specs = (P("row", "col", None, None), P())
    return jax.shard_map(
        per_device, mesh=mesh, in_specs=in_specs, out_specs=out_specs, check_vma=False
    )
```

profile of v0, /device:TPU:1, one launch (start us, length us, event | category | flops | bytes accessed | tf_op | source)
XLA Modules:
  0.0 680.2 jit_solution(9202901547140222061)
XLA Ops:
  8.0 3.2 broadcast_select_fusion.1
  12.0 19.4 %all-gather.1 = s32[16,8,2]{1,2,0:T(2,128)S(1)} all-gather(s32[1,8,2]{1,2,0:T(2,128)S(1)} %bitcast.109), channel_id=1, replica_groups=mesh['row'=16,'col'=8] {'row'}, dimensions={0}, use_global_device_ids=true | all-gather | bytes 1088 | tf_op jit(solution)/shard_map/all_gather | solution.py:22
  31.6 17.7 %all-gather = s32[8,2,8]{2,1,0:T(2,128)S(1)} all-gather(s32[1,2,8]{2,1,0:T(2,128)S(1)} %bitcast.110), channel_id=1, replica_groups=mesh['row'=16,'col'=8] {'col'}, dimensions={0}, use_global_device_ids=true | all-gather | bytes 576 | tf_op jit(solution)/shard_map/all_gather | solution.py:18
  49.5 50.6 %all-gather.7.cloned.1.call-done = bf16[8,16,256,256]{3,2,1,0:T(8,128)(2,1)} async-done(((bf16[8,2,256,256]{3,2,1,0:T(8,128)(2,1)}), bf16[8,16,256,256]{3,2,1,0:T(8,128)(2,1)}) %all-gather.7.cloned.1.call-update) | async-done | bytes 16777232 | tf_op jit(solution)/shard_map/all_gather | solution.py:17
  100.1 198.9 %all-gather.5.cloned.1.call-done = bf16[128,2,256,256]{3,2,1,0:T(8,128)(2,1)} async-done(((bf16[8,2,256,256]{3,2,1,0:T(8,128)(2,1)}), bf16[128,2,256,256]{3,2,1,0:T(8,128)(2,1)}) %all-gather.5.cloned.1.call-update) | async-done | bytes 33554448 | tf_op jit(solution)/shard_map/all_gather | solution.py:21
  299.0 307.8 %while.12 = (s32[]{:T(128)}, bf16[8,4,256,256]{3,2,1,0:T(8,128)(2,1)}, f32[8]{0:T(128)S(1)}, s32[8]{0:T(128)S(1)}, pred[8]{0:T(512)(128)(4,1)S(1)}, /*index=5*/s...) while((s32[]{:T(128)}, ...), condition=%wide.region_3.4_spmd, body=%wide.region_0.3_spmd.sunk | while | flops 1177093376 | bytes 52828456 | solution.py:56
  301.5 4.9 gather_fusion.1
  306.4 7.4 %convolution_bitcast_fusion.2 = f32[16,2,256,256]{2,3,1,0:T(8,128)} fusion(bf16[16,2,256,256]{3,2,1,0:T(8,128)(2,1)} %gather_fusion.1, bf16[8,16,256,256]{3,2,1,0:T(8,128)(2,1)} %get-tuple-element.271, s32[]{:T(128)S(6)} %select_n.86), kind=kOutput, calls=%fused_computation.5.clone.1 | convolution fusion | flops 1073741824 | bytes 14680068 | tf_op jit(solution)/shard_map/while/body/eval_jaxpr/exy,esyz->esxz/dot_general | solution.py:36
  313.8 10.2 %copy.58 = f32[4,8,256,256]{3,1,2,0:T(8,128)} copy(f32[4,8,256,256]{2,3,1,0:T(8,128)} %bitcast.106) | data formatting | bytes 16777216 | tf_op jit(solution)/shard_map/while
  324.9 6.1 fusion.45
  331.0 1.0 dynamic-slice_bitcast_fusion.2
  332.7 1.8 select_reduce_fusion.2
  334.5 0.9 copy_dynamic-update-slice_fusion.2
  336.6 0.7 dynamic_update_slice.12
  339.8 4.9 gather_fusion.1
  344.7 7.4 %convolution_bitcast_fusion.2 = f32[16,2,256,256]{2,3,1,0:T(8,128)} fusion(bf16[16,2,256,256]{3,2,1,0:T(8,128)(2,1)} %gather_fusion.1, bf16[8,16,256,256]{3,2,1,0:T(8,128)(2,1)} %get-tuple-element.271, s32[]{:T(128)S(6)} %select_n.86), kind=kOutput, calls=%fused_computation.5.clone.1 | convolution fusion | flops 1073741824 | bytes 14680068 | tf_op jit(solution)/shard_map/while/body/eval_jaxpr/exy,esyz->esxz/dot_general | solution.py:36
  352.1 10.2 %copy.58 = f32[4,8,256,256]{3,1,2,0:T(8,128)} copy(f32[4,8,256,256]{2,3,1,0:T(8,128)} %bitcast.106) | data formatting | bytes 16777216 | tf_op jit(solution)/shard_map/while
  363.2 6.1 fusion.45
  369.4 1.0 dynamic-slice_bitcast_fusion.2
  371.0 1.8 select_reduce_fusion.2
  372.8 0.9 copy_dynamic-update-slice_fusion.2
  378.1 4.9 gather_fusion.1
  383.0 7.4 %convolution_bitcast_fusion.2 = f32[16,2,256,256]{2,3,1,0:T(8,128)} fusion(bf16[16,2,256,256]{3,2,1,0:T(8,128)(2,1)} %gather_fusion.1, bf16[8,16,256,256]{3,2,1,0:T(8,128)(2,1)} %get-tuple-element.271, s32[]{:T(128)S(6)} %select_n.86), kind=kOutput, calls=%fused_computation.5.clone.1 | convolution fusion | flops 1073741824 | bytes 14680068 | tf_op jit(solution)/shard_map/while/body/eval_jaxpr/exy,esyz->esxz/dot_general | solution.py:36
  390.4 10.2 %copy.58 = f32[4,8,256,256]{3,1,2,0:T(8,128)} copy(f32[4,8,256,256]{2,3,1,0:T(8,128)} %bitcast.106) | data formatting | bytes 16777216 | tf_op jit(solution)/shard_map/while
  401.6 6.1 fusion.45
  407.7 1.0 dynamic-slice_bitcast_fusion.2
  409.3 1.8 select_reduce_fusion.2
  411.1 0.9 copy_dynamic-update-slice_fusion.2
  416.5 5.4 gather_fusion.1
  421.8 7.4 %convolution_bitcast_fusion.2 = f32[16,2,256,256]{2,3,1,0:T(8,128)} fusion(bf16[16,2,256,256]{3,2,1,0:T(8,128)(2,1)} %gather_fusion.1, bf16[8,16,256,256]{3,2,1,0:T(8,128)(2,1)} %get-tuple-element.271, s32[]{:T(128)S(6)} %select_n.86), kind=kOutput, calls=%fused_computation.5.clone.1 | convolution fusion | flops 1073741824 | bytes 14680068 | tf_op jit(solution)/shard_map/while/body/eval_jaxpr/exy,esyz->esxz/dot_general | solution.py:36
  429.3 10.2 %copy.58 = f32[4,8,256,256]{3,1,2,0:T(8,128)} copy(f32[4,8,256,256]{2,3,1,0:T(8,128)} %bitcast.106) | data formatting | bytes 16777216 | tf_op jit(solution)/shard_map/while
  440.4 6.1 fusion.45
  446.5 1.0 dynamic-slice_bitcast_fusion.2
  448.2 1.8 select_reduce_fusion.2
  449.9 0.9 copy_dynamic-update-slice_fusion.2
  455.3 4.9 gather_fusion.1
  460.2 7.4 %convolution_bitcast_fusion.2 = f32[16,2,256,256]{2,3,1,0:T(8,128)} fusion(bf16[16,2,256,256]{3,2,1,0:T(8,128)(2,1)} %gather_fusion.1, bf16[8,16,256,256]{3,2,1,0:T(8,128)(2,1)} %get-tuple-element.271, s32[]{:T(128)S(6)} %select_n.86), kind=kOutput, calls=%fused_computation.5.clone.1 | convolution fusion | flops 1073741824 | bytes 14680068 | tf_op jit(solution)/shard_map/while/body/eval_jaxpr/exy,esyz->esxz/dot_general | solution.py:36
  467.6 10.2 %copy.58 = f32[4,8,256,256]{3,1,2,0:T(8,128)} copy(f32[4,8,256,256]{2,3,1,0:T(8,128)} %bitcast.106) | data formatting | bytes 16777216 | tf_op jit(solution)/shard_map/while
  478.7 6.1 fusion.45
  484.8 1.0 dynamic-slice_bitcast_fusion.2
  486.5 1.8 select_reduce_fusion.2
  488.3 0.9 copy_dynamic-update-slice_fusion.2
  493.6 5.0 gather_fusion.1
  498.6 7.4 %convolution_bitcast_fusion.2 = f32[16,2,256,256]{2,3,1,0:T(8,128)} fusion(bf16[16,2,256,256]{3,2,1,0:T(8,128)(2,1)} %gather_fusion.1, bf16[8,16,256,256]{3,2,1,0:T(8,128)(2,1)} %get-tuple-element.271, s32[]{:T(128)S(6)} %select_n.86), kind=kOutput, calls=%fused_computation.5.clone.1 | convolution fusion | flops 1073741824 | bytes 14680068 | tf_op jit(solution)/shard_map/while/body/eval_jaxpr/exy,esyz->esxz/dot_general | solution.py:36
  506.1 10.2 %copy.58 = f32[4,8,256,256]{3,1,2,0:T(8,128)} copy(f32[4,8,256,256]{2,3,1,0:T(8,128)} %bitcast.106) | data formatting | bytes 16777216 | tf_op jit(solution)/shard_map/while
  517.2 6.1 fusion.45
  523.3 1.0 dynamic-slice_bitcast_fusion.2
  524.9 1.8 select_reduce_fusion.2
  526.7 0.9 copy_dynamic-update-slice_fusion.2
  532.1 5.0 gather_fusion.1
  537.1 7.4 %convolution_bitcast_fusion.2 = f32[16,2,256,256]{2,3,1,0:T(8,128)} fusion(bf16[16,2,256,256]{3,2,1,0:T(8,128)(2,1)} %gather_fusion.1, bf16[8,16,256,256]{3,2,1,0:T(8,128)(2,1)} %get-tuple-element.271, s32[]{:T(128)S(6)} %select_n.86), kind=kOutput, calls=%fused_computation.5.clone.1 | convolution fusion | flops 1073741824 | bytes 14680068 | tf_op jit(solution)/shard_map/while/body/eval_jaxpr/exy,esyz->esxz/dot_general | solution.py:36
  544.6 10.2 %copy.58 = f32[4,8,256,256]{3,1,2,0:T(8,128)} copy(f32[4,8,256,256]{2,3,1,0:T(8,128)} %bitcast.106) | data formatting | bytes 16777216 | tf_op jit(solution)/shard_map/while
  555.7 6.1 fusion.45
  561.8 1.0 dynamic-slice_bitcast_fusion.2
  563.4 1.8 select_reduce_fusion.2
  565.2 0.9 copy_dynamic-update-slice_fusion.2
  570.6 5.3 gather_fusion.1
  575.8 7.4 %convolution_bitcast_fusion.2 = f32[16,2,256,256]{2,3,1,0:T(8,128)} fusion(bf16[16,2,256,256]{3,2,1,0:T(8,128)(2,1)} %gather_fusion.1, bf16[8,16,256,256]{3,2,1,0:T(8,128)(2,1)} %get-tuple-element.271, s32[]{:T(128)S(6)} %select_n.86), kind=kOutput, calls=%fused_computation.5.clone.1 | convolution fusion | flops 1073741824 | bytes 14680068 | tf_op jit(solution)/shard_map/while/body/eval_jaxpr/exy,esyz->esxz/dot_general | solution.py:36
  583.3 10.2 %copy.58 = f32[4,8,256,256]{3,1,2,0:T(8,128)} copy(f32[4,8,256,256]{2,3,1,0:T(8,128)} %bitcast.106) | data formatting | bytes 16777216 | tf_op jit(solution)/shard_map/while
  594.4 6.1 fusion.45
  600.5 1.0 dynamic-slice_bitcast_fusion.2
  602.2 1.8 select_reduce_fusion.2
  603.9 0.9 copy_dynamic-update-slice_fusion.2
  607.4 66.0 %psum.7 = f32[1]{0:T(128)} all-reduce(f32[1]{0:T(128)} %bitcast.24), channel_id=1, replica_groups=mesh['row'=16,'col'=8] {'row','col'}, use_global_device_ids=true, to_apply=%region_5.6 | all-reduce | flops 1 | bytes 8 | tf_op jit(solution)/shard_map/psum | solution.py:57
  (140 shorter events, 29.5 us)
Async XLA Ops:
  7.2 93.0 %all-gather.7.cloned.1.call-start = ((), (), s32[]{:S(2)}) async-start(), calls=%async_computation.1 | async-start | bytes 18874368 | tf_op jit(solution)/shard_map/all_gather | solution.py:17
  8.0 4.0 copy-start
  8.0 41.4 %copy-start.1 = (s32[8,4]{0,1:T(4,128)S(1)}, s32[8,4]{0,1:T(4,128)}, u32[]{:S(2)}) copy-start(s32[8,4]{0,1:T(4,128)} %param.8) | copy-start | bytes 388
  8.0 41.5 %copy-start.2 = (s32[8]{0:T(128)S(1)}, s32[8]{0:T(128)}, u32[]{:S(2)}) copy-start(s32[8]{0:T(128)} %param.9) | copy-start | bytes 100
  11.2 287.8 %all-gather.5.cloned.1.call-start = ((), (), s32[]{:S(2)}) async-start(), calls=%async_computation | async-start | bytes 35651584 | tf_op jit(solution)/shard_map/all_gather | solution.py:21
Sparse Core Ops, SparseCore 0:
  11.3 88.7 all-gather.6
  102.3 196.6 all-gather.4
where the time goes:
time: 683 us; the launch traced here: 680 us
  waiting for transfers between devices  250 us (37%)
  local copies, waits for them, and re-layouts  159 us (23%)
  matrix products  123 us (18%)
  blocking collectives  103 us (15%)
  loops' own time  20.5 us (3%)
  between operations  14.1 us (2%)
  other arithmetic  10 us (1%)
    all_gather x1, waiting for transfers between devices, per_device(): lax.all_gather(cleared, 'row', axis=0, tiled=True)  199 us
    while x16, local copies, waits for them, and re-layouts  89.7 us
    psum x1, blocking collectives, per_device(): trace_total = lax.psum(jnp.sum(parts), ('row', 'col'))  66 us
    dot_general x8, matrix products, one_row(): jnp.einsum('exy,esyz->esxz', lhs, fetched, preferred_element_type=jnp.flo...  59.5 us
    all_gather x1, waiting for transfers between devices, per_device(): lax.all_gather(cleared, 'col', axis=1, tiled=True)  50.6 us
    dot_general x8, matrix products, one_row(): jnp.dot(match, products.reshape(width, block * block), precision=lax.Prec...  49 us
    gather x8, local copies, waits for them, and re-layouts, fetch(): fetched = right_blocks[source_rows]  40.2 us
    another operation x1, loops' own time, per_device(): purified, parts = lax.map(one_row, jnp.arange(rows, dtype=jnp.int32))  20.5 us
  transfers between devices with their start and end apart: 2, of which 2 were waited for; matrix products, arithmetic and copies ran while one was open for 0% of the time, Pallas kernels for 0%

commit v1 on v0

--- a/solution.py
+++ b/solution.py
@@ -14,7 +14,9 @@
     flag_rows = branch_flag == 1
     base_row = lax.axis_index("row") * rows
     left_blocks, left_cols = (
-        lax.all_gather(cleared, "col", axis=1, tiled=True),
+        jnp.concatenate(
+            lax.all_to_all(jnp.stack([cleared] * lax.axis_size("col")), "col", 0, 0), axis=1
+        ),
         lax.all_gather(x_cols, "col", axis=1, tiled=True),
     )
     right_blocks, right_cols = (

time: 683 us -> 611 us (0.89)
  waiting for transfers between devices: 250 us -> 0.02 us
  blocking collectives: 103 us -> 254 us
  local copies, waits for them, and re-layouts: 159 us -> 180 us
  starting transfers between devices: 0.08 us -> 7.15 us
    all_gather x1, waiting for transfers between devices: 199 us -> 0.01 us  [per_device(): lax.all_gather(cleared, 'row', axis=0, tiled=True)]
    all_gather x1, blocking collectives: 17.7 us -> 166 us  [per_device(): lax.all_gather(x_cols, 'col', axis=1, tiled=True)]
    all_gather x1 -> x0, waiting for transfers between devices: 50.6 us -> none  [per_device(): lax.all_gather(cleared, 'col', axis=1, tiled=True)]
    all_to_all x0 -> x1, local copies, waits for them, and re-layouts: none -> 13.9 us  [per_device(): lax.all_to_all(jnp.stack([cleared] * lax.axis_size('col')), 'col', 0, 0)]
    all_to_all x0 -> x1, starting transfers between devices: none -> 7.11 us  [per_device(): lax.all_to_all(jnp.stack([cleared] * lax.axis_size('col')), 'col', 0, 0)]
    another operation x0 -> x1, local copies, waits for them, and re-layouts: none -> 6.84 us  [per_device(): jnp.stack([cleared] * lax.axis_size('col'))]
  transfers between devices with their start and end apart: 2 -> 2, of which waited for: 2 -> 0; matrix products, arithmetic and copies ran while one was open for 0% -> 3% of each run, Pallas kernels for 0% -> 0%
where the time goes in v1:
time: 611 us; the launch traced here: 608 us
  blocking collectives  254 us (42%)
  local copies, waits for them, and re-layouts  180 us (29%)
  matrix products  123 us (20%)
  loops' own time  20.5 us (3%)
  between operations  14 us (2%)
  other arithmetic  10 us (2%)
  starting transfers between devices  7.15 us (1%)
    all_gather x1, blocking collectives, per_device(): lax.all_gather(x_cols, 'col', axis=1, tiled=True)  166 us
    while x16, local copies, waits for them, and re-layouts  89.7 us
    psum x1, blocking collectives, per_device(): trace_total = lax.psum(jnp.sum(parts), ('row', 'col'))  66.4 us
    dot_general x8, matrix products, one_row(): jnp.einsum('exy,esyz->esxz', lhs, fetched, preferred_element_type=jnp.flo...  59.5 us
    dot_general x8, matrix products, one_row(): jnp.dot(match, products.reshape(width, block * block), precision=lax.Prec...  49 us
    gather x8, local copies, waits for them, and re-layouts, fetch(): fetched = right_blocks[source_rows]  40.2 us
    all_gather x1, blocking collectives, per_device(): lax.all_gather(x_cols, 'row', axis=0, tiled=True)  21.5 us
    another operation x1, loops' own time, per_device(): purified, parts = lax.map(one_row, jnp.arange(rows, dtype=jnp.int32))  20.5 us
  transfers between devices with their start and end apart: 2, of which 0 were waited for; matrix products, arithmetic and copies ran while one was open for 3% of the time, Pallas kernels for 0%

profile of v1, /device:TPU:1, one launch (start us, length us, event | category | flops | bytes accessed | tf_op | source)
XLA Modules:
  0.0 608.3 jit_solution(7083019634689144586)
XLA Ops:
  8.0 3.1 broadcast_select_fusion.1
  11.1 6.8 %stack.2 = bf16[8,8,2,256,256]{4,3,2,1,0:T(8,128)(2,1)} broadcast(bf16[8,2,256,256]{3,2,1,0:T(8,128)(2,1)} %broadcast_select_fusion.1), dimensions={1,2,3,4} | broadcast | bytes 18874368 | tf_op jit(solution)/shard_map/stack | solution.py:18
  18.0 7.1 %all-to-all-start = ((bf16[8,8,2,256,256]{4,3,2,1,0:T(8,128)(2,1)}), bf16[8,8,2,256,256]{4,3,2,1,0:T(8,128)(2,1)}, u32[]{:S(2)}, u32[]{:S(2)}) async-start(bf16[8,8,2,256,256]{4,3,2,1,0:T(8,128)(2,1)} %stack.2), calls=%async_computation | async-start | bytes 33554432 | tf_op jit(solution)/shard_map/all_to_all | solution.py:18
  25.2 21.5 %all-gather.1 = s32[16,8,2]{1,2,0:T(2,128)S(1)} all-gather(s32[1,8,2]{1,2,0:T(2,128)S(1)} %bitcast.113), channel_id=1, replica_groups=mesh['row'=16,'col'=8] {'row'}, dimensions={0}, use_global_device_ids=true | all-gather | bytes 1088 | tf_op jit(solution)/shard_map/all_gather | solution.py:24
  46.8 165.7 %all-gather = s32[8,2,8]{2,1,0:T(2,128)S(1)} all-gather(s32[1,2,8]{2,1,0:T(2,128)S(1)} %bitcast.114), channel_id=1, replica_groups=mesh['row'=16,'col'=8] {'col'}, dimensions={0}, use_global_device_ids=true | all-gather | bytes 576 | tf_op jit(solution)/shard_map/all_gather | solution.py:20
  212.7 13.9 %copy.37 = bf16[8,8,2,256,256]{4,3,2,0,1:T(8,128)(2,1)} copy(bf16[8,8,2,256,256]{4,3,2,1,0:T(8,128)(2,1)} %all-to-all-done) | data formatting | bytes 33554432 | tf_op jit(solution)/shard_map/all_to_all | solution.py:18
  226.6 307.8 %while.12 = (s32[]{:T(128)}, bf16[8,4,256,256]{3,2,1,0:T(8,128)(2,1)}, f32[8]{0:T(128)S(1)}, s32[8]{0:T(128)S(1)}, pred[8]{0:T(512)(128)(4,1)S(1)}, /*index=5*/s...) while((s32[]{:T(128)}, ...), condition=%wide.region_3.4_spmd, body=%wide.region_0.3_spmd.sunk | while | flops 1177093376 | bytes 52828456 | solution.py:58
  229.1 4.9 gather_fusion.1
  234.0 7.4 %convolution_bitcast_fusion.2 = f32[16,2,256,256]{2,3,1,0:T(8,128)} fusion(bf16[16,2,256,256]{3,2,1,0:T(8,128)(2,1)} %gather_fusion.1, bf16[8,16,256,256]{3,2,1,0:T(8,128)(2,1)} %get-tuple-element.286, s32[]{:T(128)S(6)} %select_n.86), kind=kOutput, calls=%fused_computation.5.clone.1 | convolution fusion | flops 1073741824 | bytes 14680068 | tf_op jit(solution)/shard_map/while/body/eval_jaxpr/exy,esyz->esxz/dot_general | solution.py:38
  241.4 10.2 %copy.69 = f32[4,8,256,256]{3,1,2,0:T(8,128)} copy(f32[4,8,256,256]{2,3,1,0:T(8,128)} %bitcast.109) | data formatting | bytes 16777216 | tf_op jit(solution)/shard_map/while
  252.5 6.1 %fusion.45 = f32[4,256,256]{2,0,1:T(4,128)S(1)} fusion(s32[32]{0:T(128)S(1)} %broadcast_select_fusion.3, s32[4]{0:T(128)S(1)} %fusion.44, f32[4,8,256,256]{3,1,2,0:T(8,128)} %copy.69), kind=kOutput, calls=%fused_computation.2.clone.1 | convolution fusion | flops 100663424 | bytes 9437328 | tf_op jit(solution)/shard_map/while/body/eval_jaxpr/dot_general | solution.py:45
  258.7 1.0 dynamic-slice_bitcast_fusion.2
  260.3 1.8 select_reduce_fusion.2
  262.1 0.9 copy_dynamic-update-slice_fusion.2
  267.4 4.9 gather_fusion.1
  272.3 7.4 %convolution_bitcast_fusion.2 = f32[16,2,256,256]{2,3,1,0:T(8,128)} fusion(bf16[16,2,256,256]{3,2,1,0:T(8,128)(2,1)} %gather_fusion.1, bf16[8,16,256,256]{3,2,1,0:T(8,128)(2,1)} %get-tuple-element.286, s32[]{:T(128)S(6)} %select_n.86), kind=kOutput, calls=%fused_computation.5.clone.1 | convolution fusion | flops 1073741824 | bytes 14680068 | tf_op jit(solution)/shard_map/while/body/eval_jaxpr/exy,esyz->esxz/dot_general | solution.py:38
  279.8 10.2 %copy.69 = f32[4,8,256,256]{3,1,2,0:T(8,128)} copy(f32[4,8,256,256]{2,3,1,0:T(8,128)} %bitcast.109) | data formatting | bytes 16777216 | tf_op jit(solution)/shard_map/while
  290.9 6.1 %fusion.45 = f32[4,256,256]{2,0,1:T(4,128)S(1)} fusion(s32[32]{0:T(128)S(1)} %broadcast_select_fusion.3, s32[4]{0:T(128)S(1)} %fusion.44, f32[4,8,256,256]{3,1,2,0:T(8,128)} %copy.69), kind=kOutput, calls=%fused_computation.2.clone.1 | convolution fusion | flops 100663424 | bytes 9437328 | tf_op jit(solution)/shard_map/while/body/eval_jaxpr/dot_general | solution.py:45
  297.0 1.0 dynamic-slice_bitcast_fusion.2
  298.6 1.8 select_reduce_fusion.2
  300.4 0.9 copy_dynamic-update-slice_fusion.2
  305.8 4.9 gather_fusion.1
  310.6 7.4 %convolution_bitcast_fusion.2 = f32[16,2,256,256]{2,3,1,0:T(8,128)} fusion(bf16[16,2,256,256]{3,2,1,0:T(8,128)(2,1)} %gather_fusion.1, bf16[8,16,256,256]{3,2,1,0:T(8,128)(2,1)} %get-tuple-element.286, s32[]{:T(128)S(6)} %select_n.86), kind=kOutput, calls=%fused_computation.5.clone.1 | convolution fusion | flops 1073741824 | bytes 14680068 | tf_op jit(solution)/shard_map/while/body/eval_jaxpr/exy,esyz->esxz/dot_general | solution.py:38
  318.1 10.2 %copy.69 = f32[4,8,256,256]{3,1,2,0:T(8,128)} copy(f32[4,8,256,256]{2,3,1,0:T(8,128)} %bitcast.109) | data formatting | bytes 16777216 | tf_op jit(solution)/shard_map/while
  329.2 6.1 %fusion.45 = f32[4,256,256]{2,0,1:T(4,128)S(1)} fusion(s32[32]{0:T(128)S(1)} %broadcast_select_fusion.3, s32[4]{0:T(128)S(1)} %fusion.44, f32[4,8,256,256]{3,1,2,0:T(8,128)} %copy.69), kind=kOutput, calls=%fused_computation.2.clone.1 | convolution fusion | flops 100663424 | bytes 9437328 | tf_op jit(solution)/shard_map/while/body/eval_jaxpr/dot_general | solution.py:45
  335.3 1.0 dynamic-slice_bitcast_fusion.2
  337.0 1.8 select_reduce_fusion.2
  338.7 0.9 copy_dynamic-update-slice_fusion.2
  344.1 5.4 gather_fusion.1
  349.5 7.4 %convolution_bitcast_fusion.2 = f32[16,2,256,256]{2,3,1,0:T(8,128)} fusion(bf16[16,2,256,256]{3,2,1,0:T(8,128)(2,1)} %gather_fusion.1, bf16[8,16,256,256]{3,2,1,0:T(8,128)(2,1)} %get-tuple-element.286, s32[]{:T(128)S(6)} %select_n.86), kind=kOutput, calls=%fused_computation.5.clone.1 | convolution fusion | flops 1073741824 | bytes 14680068 | tf_op jit(solution)/shard_map/while/body/eval_jaxpr/exy,esyz->esxz/dot_general | solution.py:38
  356.9 10.2 %copy.69 = f32[4,8,256,256]{3,1,2,0:T(8,128)} copy(f32[4,8,256,256]{2,3,1,0:T(8,128)} %bitcast.109) | data formatting | bytes 16777216 | tf_op jit(solution)/shard_map/while
  368.0 6.1 %fusion.45 = f32[4,256,256]{2,0,1:T(4,128)S(1)} fusion(s32[32]{0:T(128)S(1)} %broadcast_select_fusion.3, s32[4]{0:T(128)S(1)} %fusion.44, f32[4,8,256,256]{3,1,2,0:T(8,128)} %copy.69), kind=kOutput, calls=%fused_computation.2.clone.1 | convolution fusion | flops 100663424 | bytes 9437328 | tf_op jit(solution)/shard_map/while/body/eval_jaxpr/dot_general | solution.py:45
  374.2 1.0 dynamic-slice_bitcast_fusion.2
  375.8 1.8 select_reduce_fusion.2
  377.6 0.9 copy_dynamic-update-slice_fusion.2
  382.9 4.9 gather_fusion.1
  387.8 7.4 %convolution_bitcast_fusion.2 = f32[16,2,256,256]{2,3,1,0:T(8,128)} fusion(bf16[16,2,256,256]{3,2,1,0:T(8,128)(2,1)} %gather_fusion.1, bf16[8,16,256,256]{3,2,1,0:T(8,128)(2,1)} %get-tuple-element.286, s32[]{:T(128)S(6)} %select_n.86), kind=kOutput, calls=%fused_computation.5.clone.1 | convolution fusion | flops 1073741824 | bytes 14680068 | tf_op jit(solution)/shard_map/while/body/eval_jaxpr/exy,esyz->esxz/dot_general | solution.py:38
  395.2 10.2 %copy.69 = f32[4,8,256,256]{3,1,2,0:T(8,128)} copy(f32[4,8,256,256]{2,3,1,0:T(8,128)} %bitcast.109) | data formatting | bytes 16777216 | tf_op jit(solution)/shard_map/while
  406.4 6.1 %fusion.45 = f32[4,256,256]{2,0,1:T(4,128)S(1)} fusion(s32[32]{0:T(128)S(1)} %broadcast_select_fusion.3, s32[4]{0:T(128)S(1)} %fusion.44, f32[4,8,256,256]{3,1,2,0:T(8,128)} %copy.69), kind=kOutput, calls=%fused_computation.2.clone.1 | convolution fusion | flops 100663424 | bytes 9437328 | tf_op jit(solution)/shard_map/while/body/eval_jaxpr/dot_general | solution.py:45
  412.5 1.0 dynamic-slice_bitcast_fusion.2
  414.1 1.8 select_reduce_fusion.2
  415.9 0.9 copy_dynamic-update-slice_fusion.2
  421.2 5.0 gather_fusion.1
  426.3 7.4 %convolution_bitcast_fusion.2 = f32[16,2,256,256]{2,3,1,0:T(8,128)} fusion(bf16[16,2,256,256]{3,2,1,0:T(8,128)(2,1)} %gather_fusion.1, bf16[8,16,256,256]{3,2,1,0:T(8,128)(2,1)} %get-tuple-element.286, s32[]{:T(128)S(6)} %select_n.86), kind=kOutput, calls=%fused_computation.5.clone.1 | convolution fusion | flops 1073741824 | bytes 14680068 | tf_op jit(solution)/shard_map/while/body/eval_jaxpr/exy,esyz->esxz/dot_general | solution.py:38
  433.7 10.2 %copy.69 = f32[4,8,256,256]{3,1,2,0:T(8,128)} copy(f32[4,8,256,256]{2,3,1,0:T(8,128)} %bitcast.109) | data formatting | bytes 16777216 | tf_op jit(solution)/shard_map/while
  444.8 6.1 %fusion.45 = f32[4,256,256]{2,0,1:T(4,128)S(1)} fusion(s32[32]{0:T(128)S(1)} %broadcast_select_fusion.3, s32[4]{0:T(128)S(1)} %fusion.44, f32[4,8,256,256]{3,1,2,0:T(8,128)} %copy.69), kind=kOutput, calls=%fused_computation.2.clone.1 | convolution fusion | flops 100663424 | bytes 9437328 | tf_op jit(solution)/shard_map/while/body/eval_jaxpr/dot_general | solution.py:45
  451.0 1.0 dynamic-slice_bitcast_fusion.2
  452.6 1.8 select_reduce_fusion.2
  454.4 0.9 copy_dynamic-update-slice_fusion.2
  459.7 5.0 gather_fusion.1
  464.8 7.4 %convolution_bitcast_fusion.2 = f32[16,2,256,256]{2,3,1,0:T(8,128)} fusion(bf16[16,2,256,256]{3,2,1,0:T(8,128)(2,1)} %gather_fusion.1, bf16[8,16,256,256]{3,2,1,0:T(8,128)(2,1)} %get-tuple-element.286, s32[]{:T(128)S(6)} %select_n.86), kind=kOutput, calls=%fused_computation.5.clone.1 | convolution fusion | flops 1073741824 | bytes 14680068 | tf_op jit(solution)/shard_map/while/body/eval_jaxpr/exy,esyz->esxz/dot_general | solution.py:38
  472.2 10.2 %copy.69 = f32[4,8,256,256]{3,1,2,0:T(8,128)} copy(f32[4,8,256,256]{2,3,1,0:T(8,128)} %bitcast.109) | data formatting | bytes 16777216 | tf_op jit(solution)/shard_map/while
  483.3 6.1 %fusion.45 = f32[4,256,256]{2,0,1:T(4,128)S(1)} fusion(s32[32]{0:T(128)S(1)} %broadcast_select_fusion.3, s32[4]{0:T(128)S(1)} %fusion.44, f32[4,8,256,256]{3,1,2,0:T(8,128)} %copy.69), kind=kOutput, calls=%fused_computation.2.clone.1 | convolution fusion | flops 100663424 | bytes 9437328 | tf_op jit(solution)/shard_map/while/body/eval_jaxpr/dot_general | solution.py:45
  489.5 1.0 dynamic-slice_bitcast_fusion.2
  491.1 1.8 select_reduce_fusion.2
  492.9 0.9 copy_dynamic-update-slice_fusion.2
  498.2 5.3 gather_fusion.1
  503.5 7.4 %convolution_bitcast_fusion.2 = f32[16,2,256,256]{2,3,1,0:T(8,128)} fusion(bf16[16,2,256,256]{3,2,1,0:T(8,128)(2,1)} %gather_fusion.1, bf16[8,16,256,256]{3,2,1,0:T(8,128)(2,1)} %get-tuple-element.286, s32[]{:T(128)S(6)} %select_n.86), kind=kOutput, calls=%fused_computation.5.clone.1 | convolution fusion | flops 1073741824 | bytes 14680068 | tf_op jit(solution)/shard_map/while/body/eval_jaxpr/exy,esyz->esxz/dot_general | solution.py:38
  510.9 10.2 %copy.69 = f32[4,8,256,256]{3,1,2,0:T(8,128)} copy(f32[4,8,256,256]{2,3,1,0:T(8,128)} %bitcast.109) | data formatting | bytes 16777216 | tf_op jit(solution)/shard_map/while
  522.0 6.1 %fusion.45 = f32[4,256,256]{2,0,1:T(4,128)S(1)} fusion(s32[32]{0:T(128)S(1)} %broadcast_select_fusion.3, s32[4]{0:T(128)S(1)} %fusion.44, f32[4,8,256,256]{3,1,2,0:T(8,128)} %copy.69), kind=kOutput, calls=%fused_computation.2.clone.1 | convolution fusion | flops 100663424 | bytes 9437328 | tf_op jit(solution)/shard_map/while/body/eval_jaxpr/dot_general | solution.py:45
  528.2 1.0 dynamic-slice_bitcast_fusion.2
  529.8 1.8 select_reduce_fusion.2
  531.6 0.9 copy_dynamic-update-slice_fusion.2
  535.0 66.4 %psum.7 = f32[1]{0:T(128)} all-reduce(f32[1]{0:T(128)} %bitcast.26), channel_id=1, replica_groups=mesh['row'=16,'col'=8] {'row','col'}, use_global_device_ids=true, to_apply=%region_5.6 | all-reduce | flops 1 | bytes 8 | tf_op jit(solution)/shard_map/psum | solution.py:59
  (141 shorter events, 29.5 us)
Async XLA Ops:
  7.2 219.4 %all-gather.4.cloned.1.call-start = ((), (), s32[]{:S(2)}) async-start(), calls=%async_computation.1 | async-start | bytes 35651584 | tf_op jit(solution)/shard_map/all_gather | solution.py:23
  18.0 7.1 %copy-start = (s32[8,2]{0,1:T(2,128)S(1)}, s32[8,2]{0,1:T(2,128)}, u32[]{:S(2)}) copy-start(s32[8,2]{0,1:T(2,128)} %param.7) | copy-start | bytes 196
  18.0 194.6 %copy-start.1 = (s32[8,4]{0,1:T(4,128)S(1)}, s32[8,4]{0,1:T(4,128)}, u32[]{:S(2)}) copy-start(s32[8,4]{0,1:T(4,128)} %param.8) | copy-start | bytes 388
  18.0 194.7 %copy-start.2 = (s32[8]{0:T(128)S(1)}, s32[8]{0:T(128)}, u32[]{:S(2)}) copy-start(s32[8]{0:T(128)} %param.9) | copy-start | bytes 100
  18.0 194.7 %all-to-all-start = ((bf16[8,8,2,256,256]{4,3,2,1,0:T(8,128)(2,1)}), bf16[8,8,2,256,256]{4,3,2,1,0:T(8,128)(2,1)}, u32[]{:S(2)}, u32[]{:S(2)}) async-start(bf16[8,8,2,256,256]{4,3,2,1,0:T(8,128)(2,1)} %stack.2), calls=%async_computation | async-start | bytes 33554432 | tf_op jit(solution)/shard_map/all_to_all | solution.py:18
Sparse Core Ops, SparseCore 0:
  11.3 199.8 all-gather.3
